TPU v7x, 256 devices: a whole 4x4x8 slice. The times are simulated.
256 devices in a mesh: dp: 8 (over x, y_hi), mp: 32 (over z, y_lo, core).
Axes of the slice: x: 4, y: 4 (y_hi: 2, y_lo: 2; y = y_hi * 2 + y_lo), z: 8, core: 2. Of those that a mesh axis runs over, the one named last changes fastest.
Arguments:
- hidden: bfloat16 [64, 128, 18432], P('dp', None, 'mp'), may hold values from -400 to 400
- cotangent: bfloat16 [64, 128, 4608], P('dp', 'mp'), may hold values from -8 to 8
- w_down: bfloat16 [18432, 4608], P('mp', 'dp'), may hold values from -0.046875 to 0.046875
- lengths: int32 [64], P('dp'), may hold values from 1 to 128, 6144 in all
Outputs:
- weight_grad: float32 [18432, 4608], P('mp', 'dp')
- d_hidden: bfloat16 [64, 128, 18432], P('dp', None, 'mp')
All inputs are finite; a program needn't handle non-finite values. No bound on the sum of `lengths` on one device may be relied on, other than what follows from the above.
Results may differ from a plain program's by a relative error of at most 0.003.
Values may be sent and summed in bfloat16 or wider, within the bound.
No kernel may reach another device: no remote copies, remote signals or barrier semaphores. Data moves between devices by JAX's collectives and lax.ppermute only.
A program may use at most 256 MiB of HBM per device.

v0:
```python
import math
import jax
import jax.numpy as jnp
from jax import lax
from jax.sharding import PartitionSpec as P


def body(hidden, cotangent, w_down, lengths):
    seqs = hidden.shape[0]
    whole = lax.all_gather(cotangent, "mp", axis=1, tiled=True)
    seq_len = whole.shape[1]
    width = whole.shape[2]
    positions = jnp.arange(seq_len, dtype=jnp.int32)
    keep = positions[None, :] < lengths[:, None]
    masked = jnp.where(keep[:, :, None], whole, jnp.zeros((), whole.dtype))
    flat = masked.reshape(seqs * seq_len, width)
    units = hidden.shape[2]
    part = flat
    grads_in = lax.dot_general(
        part,
        lax.all_gather(w_down, "dp", axis=1, tiled=True),
        (((1,), (1,)), ((), ())),
        preferred_element_type=jnp.float32,
    )
    d_hidden = grads_in.astype(jnp.bfloat16).reshape(seqs, seq_len, units)
    cot_gram = jnp.einsum("bsd,btd->bst", masked, masked, preferred_element_type=jnp.float32)
    hid_gram = jnp.einsum("bsf,btf->bst", hidden, hidden, preferred_element_type=jnp.float32)
    summed = lax.psum(hid_gram.astype(jnp.bfloat16), "mp").astype(jnp.float32)
    sq_norm = jnp.sum(summed * cot_gram, axis=(1, 2))
    full_units = units * lax.axis_size("mp")
    groups = lax.axis_size("dp")
    radius = math.sqrt(full_units * width / (seqs * groups))
    clip_scale = radius / jnp.sqrt(sq_norm + 1e-06)
    share = width // groups
    running = jnp.zeros((share * lax.axis_size("dp"), units), jnp.float32)
    for which in range(seqs):
        part = masked[which]
        running = running + clip_scale[which] * lax.dot_general(
            part, hidden[which], (((0,), (0,)), ((), ())), preferred_element_type=jnp.float32
        )
    local = lax.psum_scatter(running, "dp", scatter_dimension=0, tiled=True)
    weight_grad = local.T
    return (weight_grad, d_hidden)


def solution(mesh):
    in_specs = (P("dp", None, "mp"), P("dp", "mp", None), P("mp", "dp"), P("dp"))
    out_specs = (P("mp", "dp"), P("dp", None, "mp"))
    return jax.shard_map(body, mesh=mesh, in_specs=in_specs, out_specs=out_specs, check_vma=False)
```

profile of v0, /device:TPU:1, one launch (start us, length us, event | category | flops | bytes accessed | tf_op | source)
XLA Modules:
  0.0 570.3 jit_solution(3020541415049871727)
XLA Ops:
  7.2 1.7 copy.14
  9.0 0.0 all-reduce.2.cloned.1.call-start
  9.0 3.0 convolution_convert_fusion.1
  12.1 2.3 copy.16
  14.4 0.0 reduce-scatter.2.cloned.1.call-start
  14.4 0.7 iota_compare_fusion
  15.1 71.8 %all-gather.3.cloned.1.call-done = bf16[8,128,4608]{2,0,1:T(8,128)(2,1)} async-done(((bf16[8,4,4608]{2,0,1:T(8,128)(2,1)}), bf16[8,128,4608]{2,0,1:T(8,128)(2,1)}) %all-gather.3.cloned.1.call-update) | async-done | bytes 9437200 | tf_op jit(solution)/shard_map/all_gather | solution.py:10
  86.9 13.3 %copy_select_fusion = bf16[8,128,4608]{2,1,0:T(8,128)(2,1)} fusion(bf16[8,128,4608]{2,0,1:T(8,128)(2,1)} %all-gather.3.cloned.1.call-done, pred[8,128]{1,0:T(8,128)(4,1)S(1)} %iota_compare_fusion), kind=kLoop, calls=%fused_computation.1 | loop fusion | flops 4718592 | bytes 18875392 | tf_op jit(solution)/shard_map/jit(_where)/select_n | solution.py:15
  100.2 215.5 %all-reduce.2.cloned.1.call-done = bf16[8,128,128]{2,1,0:T(8,128)(2,1)} async-done(((bf16[8,128,128]{2,1,0:T(8,128)(2,1)}), bf16[8,128,128]{2,1,0:T(8,128)(2,1)}) %all-reduce.2.cloned.1.call-update) | async-done | bytes 262160 | tf_op jit(solution)/shard_map/psum | solution.py:28
  315.7 9.1 %fusion.8 = f32[8]{0:T(128)S(1)} fusion(bf16[8,128,4608]{2,1,0:T(8,128)(2,1)} %copy_select_fusion, bf16[8,128,128]{2,1,0:T(8,128)(2,1)} %all-reduce.2.cloned.1.call-done), kind=kOutput, calls=%fused_computation.22 | convolution fusion | flops 1208352768 | bytes 9699360 | tf_op jit(solution)/shard_map/bsd,btd->bst/dot_general | solution.py:26
  324.7 0.7 fusion.25
  325.4 7.9 %fusion.1 = f32[4608,576]{1,0:T(8,128)} fusion(bf16[8,128,4608]{2,1,0:T(8,128)(2,1)} %copy_select_fusion, bf16[8,128,576]{1,2,0:T(8,128)(2,1)S(1)} %copy-done), kind=kOutput, calls=%fused_computation.9 | convolution fusion | flops 679477248 | bytes 11943936 | tf_op jit(solution)/shard_map/dot_general | solution.py:38
  333.4 6.1 %fusion.2 = f32[4608,576]{1,0:T(8,128)} fusion(bf16[8,128,4608]{2,1,0:T(8,128)(2,1)S(1)} %bitcast.71, bf16[8,128,576]{1,2,0:T(8,128)(2,1)S(1)} %copy-done), kind=kOutput, calls=%fused_computation.11 | convolution fusion | flops 679477248 | bytes 11943936 | tf_op jit(solution)/shard_map/dot_general | solution.py:38
  339.5 6.2 %fusion.3 = f32[4608,576]{1,0:T(8,128)} fusion(bf16[8,128,4608]{2,1,0:T(8,128)(2,1)S(1)} %bitcast.71, bf16[8,128,576]{1,2,0:T(8,128)(2,1)S(1)} %copy-done), kind=kOutput, calls=%fused_computation.13 | convolution fusion | flops 679477248 | bytes 11943936 | tf_op jit(solution)/shard_map/dot_general | solution.py:38
  345.7 6.0 %fusion.4 = f32[4608,576]{1,0:T(8,128)} fusion(bf16[8,128,4608]{2,1,0:T(8,128)(2,1)S(1)} %bitcast.71, bf16[8,128,576]{1,2,0:T(8,128)(2,1)S(1)} %copy-done), kind=kOutput, calls=%fused_computation.15 | convolution fusion | flops 679477248 | bytes 11943936 | tf_op jit(solution)/shard_map/dot_general | solution.py:38
  351.7 6.1 %fusion.5 = f32[4608,576]{1,0:T(8,128)} fusion(bf16[8,128,4608]{2,1,0:T(8,128)(2,1)S(1)} %bitcast.71, bf16[8,128,576]{1,2,0:T(8,128)(2,1)S(1)} %copy-done), kind=kOutput, calls=%fused_computation.17 | convolution fusion | flops 679477248 | bytes 11943936 | tf_op jit(solution)/shard_map/dot_general | solution.py:38
  357.7 6.4 %fusion.6 = f32[4608,576]{1,0:T(8,128)} fusion(bf16[8,128,4608]{2,1,0:T(8,128)(2,1)S(1)} %bitcast.71, bf16[8,128,576]{1,2,0:T(8,128)(2,1)S(1)} %copy-done), kind=kOutput, calls=%fused_computation.19 | convolution fusion | flops 679477248 | bytes 11943936 | tf_op jit(solution)/shard_map/dot_general | solution.py:38
  364.1 6.0 %fusion.7 = f32[4608,576]{1,0:T(8,128)} fusion(bf16[8,128,4608]{2,1,0:T(8,128)(2,1)S(1)} %bitcast.71, bf16[8,128,576]{1,2,0:T(8,128)(2,1)S(1)} %copy-done), kind=kOutput, calls=%fused_computation.21 | convolution fusion | flops 679477248 | bytes 11943936 | tf_op jit(solution)/shard_map/dot_general | solution.py:38
  370.1 37.4 %multiply_add_fusion = f32[4608,576]{1,0:T(8,128)} fusion(f32[4608,576]{1,0:T(8,128)} %fusion.1, f32[4608,576]{1,0:T(8,128)} %fusion.2, f32[4608,576]{1,0:T(8,128)} %fusion.3, f32[4608,576]{1,0:T(8,128)} %fusion.4, f32[4608,576]{1,0:T(8,128)} %fusion.5, f32[4608,576]{1,0:T(8,128)} %fusion.6, f32[4608,576]{1,0:T(8,128)} %fusion.7, f32[]{:T(128)} %bitcast.21, ...), kind=kOutput, calls=%fused_computation | convolution fusion | flops 719290368 | bytes 94523392 | tf_op jit(solution)/shard_map/dot_general | solution.py:38
  407.6 1.7 all-gather.5.cloned.1.call-done
  409.3 10.1 %fusion = bf16[72,8,8,128]{3,2,1,0:T(8,128)(2,1)S(1)} fusion(bf16[1024,4608]{1,0:T(8,128)(2,1)} %bitcast.69, bf16[576,4608]{0,1:T(8,128)(2,1)} %all-gather.5.cloned.1.call-done), kind=kOutput, calls=%fused_computation.3 | convolution fusion | flops 5436407808 | bytes 15925248 | tf_op jit(solution)/shard_map/dot_general | solution.py:19
  419.4 1.2 copy.22
  420.6 140.2 %reduce-scatter.2.cloned.1.call-done = f32[576,576]{1,0:T(8,128)} async-done(((f32[4608,576]{1,0:T(8,128)}), f32[576,576]{1,0:T(8,128)}) %reduce-scatter.2.cloned.1.call-update) | async-done | bytes 1327120 | tf_op jit(solution)/shard_map/reduce_scatter | solution.py:41
  560.8 3.0 copy.17
  (16 shorter events, 0.2 us)
Async XLA Ops:
  7.2 79.8 %all-gather.3.cloned.1.call-start = ((), (), s32[]{:S(2)}) async-start(), calls=%async_computation.2 | async-start | bytes 9732096 | tf_op jit(solution)/shard_map/all_gather | solution.py:10
  9.0 306.7 %all-reduce.2.cloned.1.call-start = ((), (), s32[]{:S(2)}) async-start(), calls=%async_computation.1 | async-start | bytes 524288 | tf_op jit(solution)/shard_map/psum | solution.py:28
  12.0 397.3 %all-gather.5.cloned.1.call-start = ((), (), s32[]{:S(2)}) async-start(), calls=%async_computation.4 | async-start | bytes 6635520 | tf_op jit(solution)/shard_map/all_gather | solution.py:21
  14.4 546.5 %reduce-scatter.2.cloned.1.call-start = ((), (), s32[]{:S(2)}) async-start(), calls=%async_computation.3 | async-start | bytes 13271040 | tf_op jit(solution)/shard_map/reduce_scatter | solution.py:41
  100.2 225.2 %copy-start = (bf16[8,128,576]{1,2,0:T(8,128)(2,1)S(1)}, bf16[8,128,576]{1,2,0:T(8,128)(2,1)}, u32[]{:S(2)}) copy-start(bf16[8,128,576]{1,2,0:T(8,128)(2,1)} %param.4) | copy-start | bytes 3538948
  324.7 8.6 %slice-start = ((s8[9437184]{0:T(1024)(128)(4,1)}), s8[4194304]{0:T(1024)(128)(4,1)S(1)}, s32[]{:S(2)}) async-start(s8[9437184]{0:T(1024)(128)(4,1)} %bitcast.70), calls=%async_computation.5 | async-start | bytes 8388608
  325.4 7.9 %slice-start.1 = ((s8[9437184]{0:T(1024)(128)(4,1)}), s8[4194304]{0:T(1024)(128)(4,1)S(1)}, s32[]{:S(2)}) async-start(s8[9437184]{0:T(1024)(128)(4,1)} %bitcast.70), calls=%async_computation.6 | async-start | bytes 8388608
  325.4 7.9 %slice-start.2 = ((s8[9437184]{0:T(1024)(128)(4,1)}), s8[1048576]{0:T(1024)(128)(4,1)S(1)}, s32[]{:S(2)}) async-start(s8[9437184]{0:T(1024)(128)(4,1)} %bitcast.70), calls=%async_computation.7 | async-start | bytes 2097152
Sparse Core Ops, SparseCore 0:
  10.4 76.4 all-gather.2
  89.5 226.0 all-reduce.1
  318.8 90.3 all-gather.4
  413.3 147.4 reduce-scatter.1
where the time goes:
time: 571 us; the launch traced here: 570 us
  waiting for transfers between devices  429 us (75%)
  matrix products  104 us (18%)
  other arithmetic  14 us (2%)
  between operations  13.8 us (2%)
  local copies, waits for them, and re-layouts  8.89 us (2%)
    psum x1, waiting for transfers between devices, body(): summed = lax.psum(hid_gram.astype(jnp.bfloat16), 'mp').astype(jnp.float32)  215 us
    reduce_scatter x1, waiting for transfers between devices, body(): local = lax.psum_scatter(running, 'dp', scatter_dimension=0, tiled=True)  140 us
    dot_general x8, matrix products, body(): lax.dot_general(part, hidden[which], (((0,), (0,)), ((), ())), preferred_...  82.1 us
    all_gather x1, waiting for transfers between devices, body(): whole = lax.all_gather(cotangent, 'mp', axis=1, tiled=True)  71.8 us
    select_n x1, other arithmetic, body(): masked = jnp.where(keep[:, :, None], whole, jnp.zeros((), whole.dtype))  13.3 us
  transfers between devices with their start and end apart: 4, of which 4 were waited for; matrix products, arithmetic and copies ran while one was open for 21% of the time, Pallas kernels for 0%

commit v1 on v0

--- a/solution.py
+++ b/solution.py
@@ -25,7 +25,9 @@
     d_hidden = grads_in.astype(jnp.bfloat16).reshape(seqs, seq_len, units)
     cot_gram = jnp.einsum("bsd,btd->bst", masked, masked, preferred_element_type=jnp.float32)
     hid_gram = jnp.einsum("bsf,btf->bst", hidden, hidden, preferred_element_type=jnp.float32)
-    summed = lax.psum(hid_gram.astype(jnp.bfloat16), "mp").astype(jnp.float32)
+    summed = jnp.sum(lax.all_gather(hid_gram.astype(jnp.bfloat16), "mp"), axis=0).astype(
+        jnp.float32
+    )
     sq_norm = jnp.sum(summed * cot_gram, axis=(1, 2))
     full_units = units * lax.axis_size("mp")
     groups = lax.axis_size("dp")

time: 571 us -> 424 us (0.74)
  waiting for transfers between devices: 429 us -> 277 us
    psum x1 -> x0, waiting for transfers between devices: 215 us -> none  [body(): summed = lax.psum(hid_gram.astype(jnp.bfloat16), 'mp').astype(jnp.float32)]
    all_gather x0 -> x1, waiting for transfers between devices: none -> 71.1 us  [body(): lax.all_gather(hid_gram.astype(jnp.bfloat16), 'mp')]
  transfers between devices with their start and end apart: 4 -> 4, of which waited for: 4 -> 3; matrix products, arithmetic and copies ran while one was open for 21% -> 30% of each run, Pallas kernels for 0% -> 0%
where the time goes in v1:
time: 424 us
  waiting for transfers between devices  277 us (65%)
  matrix products  104 us (25%)
  other arithmetic  19.5 us (5%)
  between operations  13.8 us (3%)
  local copies, waits for them, and re-layouts  8.89 us (2%)
    reduce_scatter x1, waiting for transfers between devices, body(): local = lax.psum_scatter(running, 'dp', scatter_dimension=0, tiled=True)  137 us
    dot_general x8, matrix products, body(): lax.dot_general(part, hidden[which], (((0,), (0,)), ((), ())), preferred_...  81.5 us
    all_gather x1, waiting for transfers between devices, body(): lax.all_gather(hid_gram.astype(jnp.bfloat16), 'mp')  71.1 us
    all_gather x1, waiting for transfers between devices, body(): whole = lax.all_gather(cotangent, 'mp', axis=1, tiled=True)  68.5 us
    select_n x1, other arithmetic, body(): masked = jnp.where(keep[:, :, None], whole, jnp.zeros((), whole.dtype))  13.3 us
    dot_general x1, matrix products, body(): lax.dot_general(part, lax.all_gather(w_down, 'dp', axis=1, tiled=True), (...  10.1 us
    dot_general x1, matrix products, body(): jnp.einsum('bsd,btd->bst', masked, masked, preferred_element_type=jnp.flo...  9.87 us
  transfers between devices with their start and end apart: 4, of which 3 were waited for; matrix products, arithmetic and copies ran while one was open for 30% of the time, Pallas kernels for 0%

profile of v1, /device:TPU:1, one launch (start us, length us, event | category | flops | bytes accessed | tf_op | source)
XLA Modules:
  0.0 423.6 jit_solution(11371112275112001052)
XLA Ops:
  7.2 3.0 convolution_convert_fusion.1
  10.2 0.0 all-gather.5.cloned.1.call-start
  10.3 1.7 copy.14
  12.0 0.0 all-gather.7.cloned.1.call-start
  12.1 2.3 copy.16
  14.4 0.7 iota_compare_fusion
  15.1 71.1 %all-gather.9.cloned.1.call-done = bf16[256,128,128]{2,1,0:T(8,128)(2,1)} async-done(((bf16[8,128,128]{2,1,0:T(8,128)(2,1)}), bf16[256,128,128]{2,1,0:T(8,128)(2,1)}) %all-gather.9.cloned.1.call-update) | async-done | bytes 8388624 | tf_op jit(solution)/shard_map/all_gather | solution.py:28
  86.2 5.5 %reduce_sum.21 = bf16[8,128,128]{2,1,0:T(8,128)(2,1)S(1)} reduce(bf16[32,8,128,128]{3,2,1,0:T(8,128)(2,1)} %bitcast.73, bf16[]{:T(256)} %constant.2.clone.1), dimensions={0}, to_apply=%region_0.1 | reduce | flops 4063232 | bytes 8650754 | tf_op jit(solution)/shard_map/reduce_sum | solution.py:28
  91.8 68.5 %all-gather.5.cloned.1.call-done = bf16[8,128,4608]{2,0,1:T(8,128)(2,1)} async-done(((bf16[8,4,4608]{2,0,1:T(8,128)(2,1)}), bf16[8,128,4608]{2,0,1:T(8,128)(2,1)}) %all-gather.5.cloned.1.call-update) | async-done | bytes 9437200 | tf_op jit(solution)/shard_map/all_gather | solution.py:10
  160.2 13.3 %copy_select_fusion = bf16[8,128,4608]{2,1,0:T(8,128)(2,1)} fusion(bf16[8,128,4608]{2,0,1:T(8,128)(2,1)} %all-gather.5.cloned.1.call-done, pred[8,128]{1,0:T(8,128)(4,1)S(1)} %iota_compare_fusion), kind=kLoop, calls=%fused_computation.1 | loop fusion | flops 4718592 | bytes 18875392 | tf_op jit(solution)/shard_map/jit(_where)/select_n | solution.py:15
  173.5 9.9 %fusion.8 = f32[8]{0:T(128)S(1)} fusion(bf16[8,128,4608]{2,1,0:T(8,128)(2,1)} %copy_select_fusion, bf16[8,128,128]{2,1,0:T(8,128)(2,1)S(1)} %reduce_sum.21), kind=kOutput, calls=%fused_computation.22 | convolution fusion | flops 1208352768 | bytes 9699360 | tf_op jit(solution)/shard_map/bsd,btd->bst/dot_general | solution.py:26
  183.4 0.7 fusion.25
  184.1 8.0 %fusion.1 = f32[4608,576]{1,0:T(8,128)} fusion(bf16[8,128,4608]{2,1,0:T(8,128)(2,1)} %copy_select_fusion, bf16[8,128,576]{1,2,0:T(8,128)(2,1)S(1)} %copy-done), kind=kOutput, calls=%fused_computation.9 | convolution fusion | flops 679477248 | bytes 11943936 | tf_op jit(solution)/shard_map/dot_general | solution.py:40
  192.1 6.1 %fusion.2 = f32[4608,576]{1,0:T(8,128)} fusion(bf16[8,128,4608]{2,1,0:T(8,128)(2,1)S(1)} %bitcast.72, bf16[8,128,576]{1,2,0:T(8,128)(2,1)S(1)} %copy-done), kind=kOutput, calls=%fused_computation.11 | convolution fusion | flops 679477248 | bytes 11943936 | tf_op jit(solution)/shard_map/dot_general | solution.py:40
  198.2 6.0 %fusion.3 = f32[4608,576]{1,0:T(8,128)} fusion(bf16[8,128,4608]{2,1,0:T(8,128)(2,1)S(1)} %bitcast.72, bf16[8,128,576]{1,2,0:T(8,128)(2,1)S(1)} %copy-done), kind=kOutput, calls=%fused_computation.13 | convolution fusion | flops 679477248 | bytes 11943936 | tf_op jit(solution)/shard_map/dot_general | solution.py:40
  204.2 6.0 %fusion.4 = f32[4608,576]{1,0:T(8,128)} fusion(bf16[8,128,4608]{2,1,0:T(8,128)(2,1)S(1)} %bitcast.72, bf16[8,128,576]{1,2,0:T(8,128)(2,1)S(1)} %copy-done), kind=kOutput, calls=%fused_computation.15 | convolution fusion | flops 679477248 | bytes 11943936 | tf_op jit(solution)/shard_map/dot_general | solution.py:40
  210.2 6.1 %fusion.5 = f32[4608,576]{1,0:T(8,128)} fusion(bf16[8,128,4608]{2,1,0:T(8,128)(2,1)S(1)} %bitcast.72, bf16[8,128,576]{1,2,0:T(8,128)(2,1)S(1)} %copy-done), kind=kOutput, calls=%fused_computation.17 | convolution fusion | flops 679477248 | bytes 11943936 | tf_op jit(solution)/shard_map/dot_general | solution.py:40
  216.2 6.0 %fusion.6 = f32[4608,576]{1,0:T(8,128)} fusion(bf16[8,128,4608]{2,1,0:T(8,128)(2,1)S(1)} %bitcast.72, bf16[8,128,576]{1,2,0:T(8,128)(2,1)S(1)} %copy-done), kind=kOutput, calls=%fused_computation.19 | convolution fusion | flops 679477248 | bytes 11943936 | tf_op jit(solution)/shard_map/dot_general | solution.py:40
  222.2 6.0 %fusion.7 = f32[4608,576]{1,0:T(8,128)} fusion(bf16[8,128,4608]{2,1,0:T(8,128)(2,1)S(1)} %bitcast.72, bf16[8,128,576]{1,2,0:T(8,128)(2,1)S(1)} %copy-done), kind=kOutput, calls=%fused_computation.21 | convolution fusion | flops 679477248 | bytes 11943936 | tf_op jit(solution)/shard_map/dot_general | solution.py:40
  228.2 37.4 %multiply_add_fusion = f32[4608,576]{1,0:T(8,128)} fusion(f32[4608,576]{1,0:T(8,128)} %fusion.1, f32[4608,576]{1,0:T(8,128)} %fusion.2, f32[4608,576]{1,0:T(8,128)} %fusion.3, f32[4608,576]{1,0:T(8,128)} %fusion.4, f32[4608,576]{1,0:T(8,128)} %fusion.5, f32[4608,576]{1,0:T(8,128)} %fusion.6, f32[4608,576]{1,0:T(8,128)} %fusion.7, f32[]{:T(128)} %bitcast.22, ...), kind=kOutput, calls=%fused_computation | convolution fusion | flops 719290368 | bytes 94523392 | tf_op jit(solution)/shard_map/dot_general | solution.py:40
  265.7 10.1 %fusion = bf16[72,8,8,128]{3,2,1,0:T(8,128)(2,1)S(1)} fusion(bf16[1024,4608]{1,0:T(8,128)(2,1)} %bitcast.70, bf16[576,4608]{0,1:T(8,128)(2,1)} %all-gather.7.cloned.1.call-done), kind=kOutput, calls=%fused_computation.3 | convolution fusion | flops 5436407808 | bytes 15925248 | tf_op jit(solution)/shard_map/dot_general | solution.py:19
  275.8 1.2 copy.22
  277.0 137.1 %reduce-scatter.2.cloned.1.call-done = f32[576,576]{1,0:T(8,128)} async-done(((f32[4608,576]{1,0:T(8,128)}), f32[576,576]{1,0:T(8,128)}) %reduce-scatter.2.cloned.1.call-update) | async-done | bytes 1327120 | tf_op jit(solution)/shard_map/reduce_scatter | solution.py:43
  414.1 3.0 copy.17
  (17 shorter events, 0.2 us)
Async XLA Ops:
  7.2 79.1 %all-gather.9.cloned.1.call-start = ((), (), s32[]{:S(2)}) async-start(), calls=%async_computation.4 | async-start | bytes 8650752 | tf_op jit(solution)/shard_map/all_gather | solution.py:28
  10.2 150.0 %all-gather.5.cloned.1.call-start = ((), (), s32[]{:S(2)}) async-start(), calls=%async_computation.1 | async-start | bytes 9732096 | tf_op jit(solution)/shard_map/all_gather | solution.py:10
  12.0 253.6 %all-gather.7.cloned.1.call-start = ((), (), s32[]{:S(2)}) async-start(), calls=%async_computation.3 | async-start | bytes 6635520 | tf_op jit(solution)/shard_map/all_gather | solution.py:21
  14.4 399.8 %reduce-scatter.2.cloned.1.call-start = ((), (), s32[]{:S(2)}) async-start(), calls=%async_computation.2 | async-start | bytes 13271040 | tf_op jit(solution)/shard_map/reduce_scatter | solution.py:43
  173.5 10.6 %copy-start = (bf16[8,128,576]{1,2,0:T(8,128)(2,1)S(1)}, bf16[8,128,576]{1,2,0:T(8,128)(2,1)}, u32[]{:S(2)}) copy-start(bf16[8,128,576]{1,2,0:T(8,128)(2,1)} %param.4) | copy-start | bytes 3538948
  183.4 8.7 %slice-start = ((s8[9437184]{0:T(1024)(128)(4,1)}), s8[4194304]{0:T(1024)(128)(4,1)S(1)}, s32[]{:S(2)}) async-start(s8[9437184]{0:T(1024)(128)(4,1)} %bitcast.71), calls=%async_computation.5 | async-start | bytes 8388608
  184.1 8.0 %slice-start.1 = ((s8[9437184]{0:T(1024)(128)(4,1)}), s8[4194304]{0:T(1024)(128)(4,1)S(1)}, s32[]{:S(2)}) async-start(s8[9437184]{0:T(1024)(128)(4,1)} %bitcast.71), calls=%async_computation.6 | async-start | bytes 8388608
  184.1 8.0 %slice-start.2 = ((s8[9437184]{0:T(1024)(128)(4,1)}), s8[1048576]{0:T(1024)(128)(4,1)S(1)}, s32[]{:S(2)}) async-start(s8[9437184]{0:T(1024)(128)(4,1)} %bitcast.71), calls=%async_computation.7 | async-start | bytes 2097152
Sparse Core Ops, SparseCore 0:
  10.3 75.8 all-gather.8
  88.7 71.5 all-gather.4
  163.4 88.9 all-gather.6
  265.8 148.3 reduce-scatter.1
